TPU v7x, 1024 devices: a whole 4x4x32 slice. The times are simulated.
1024 devices in a mesh: ctx: 64 (over x_hi, z), fsdp: 16 (over x_lo, y, core).
Axes of the slice: x: 4 (x_hi: 2, x_lo: 2; x = x_hi * 2 + x_lo), y: 4, z: 32, core: 2. Of those that a mesh axis runs over, the one named last changes fastest.
Arguments:
- query_stream: bfloat16 [8192, 8192], P('ctx', 'fsdp'), may hold values from -6 to 6
- key_stream: bfloat16 [8192, 8192], P('ctx', 'fsdp'), may hold values from -6 to 6
- value_stream: bfloat16 [8192, 8192], P('ctx', 'fsdp'), may hold values from -6 to 6
- conv_weight: float32 [3, 3, 8192], P(None, None, 'fsdp'), may hold values from -3.5 to 3.5
- decay_rates: float32 [16, 8192], P(None, 'fsdp'), may hold values from 3.0517578e-05 to 0.05, as said below
- residues: float32 [16, 8192], P(None, 'fsdp'), may hold values from -0.31622777 to 0.31622777
- skip_gain: float32 [8192], P('fsdp'), may hold values from -4 to 4
Outputs:
- gated_output: bfloat16 [8192, 8192], P('ctx', 'fsdp')
Inputs may be any that keep to these rules, and one draw needn't show every extreme that they name: `decay_rates`: all rates are positive.
All inputs are finite; a program needn't handle non-finite values.
Results may differ from a plain program's by a relative error of at most 0.0053.
Values may be sent and summed in bfloat16 or wider, within the bound.
A program may use at most 32 MiB of HBM per device.

v0:
```python
import math

import jax
import jax.numpy as jnp
from jax import lax
from jax.sharding import PartitionSpec as P

PRECISE_SETTING = lax.Precision.HIGHEST


def dft_tables(length):
    indices = jnp.arange(length, dtype=jnp.int32)
    products = indices[:, None] * indices[None, :] % length
    angles = products.astype(jnp.float32) * (2.0 * math.pi / length)
    return (jnp.cos(angles), jnp.sin(angles))


def twist_tables(outer_len, inner_len):
    outer_idx = jnp.arange(outer_len, dtype=jnp.int32)
    inner_idx = jnp.arange(inner_len, dtype=jnp.int32)
    products = outer_idx[:, None] * inner_idx[None, :] % (outer_len * inner_len)
    angles = products.astype(jnp.float32) * (2.0 * math.pi / (outer_len * inner_len))
    return (jnp.cos(angles), jnp.sin(angles))


def transform_plan(seq_len):
    total_len = 2 * seq_len
    inner_len = math.gcd(seq_len, 2 ** ((total_len.bit_length() - 1) // 2))
    outer_len = total_len // inner_len
    return dft_tables(outer_len) + dft_tables(inner_len) + twist_tables(outer_len, inner_len)


def forward_spectrum(signal, plan):
    outer_cosine, outer_sine, cos_inner, sin_inner, twist_cos, twist_sin = plan
    outer_len = outer_cosine.shape[0]
    inner_len = cos_inner.shape[0]
    outer_half_length = outer_len // 2
    block_list = signal.reshape(signal.shape[0], outer_half_length, inner_len)
    segment_real = jnp.einsum(
        "rv,tvs->trs", outer_cosine[:, :outer_half_length], block_list, precision=PRECISE_SETTING
    )
    segment_imaginary = -jnp.einsum(
        "rv,tvs->trs", outer_sine[:, :outer_half_length], block_list, precision=PRECISE_SETTING
    )
    twist_re = segment_real * twist_cos[None] + segment_imaginary * twist_sin[None]
    twist_im = segment_imaginary * twist_cos[None] - segment_real * twist_sin[None]
    freq_re = jnp.einsum(
        "cka,ab->ckb", twist_re, cos_inner, precision=PRECISE_SETTING
    ) + jnp.einsum("cka,ab->ckb", twist_im, sin_inner, precision=PRECISE_SETTING)
    freq_im = jnp.einsum(
        "cka,ab->ckb", twist_im, cos_inner, precision=PRECISE_SETTING
    ) - jnp.einsum("cka,ab->ckb", twist_re, sin_inner, precision=PRECISE_SETTING)
    return (freq_re, freq_im)


def inverse_real(freq_re, freq_im, plan):
    outer_cosine, outer_sine, cos_inner, sin_inner, twist_cos, twist_sin = plan
    outer_len = outer_cosine.shape[0]
    inner_len = cos_inner.shape[0]
    outer_half_length = outer_len // 2
    mid_re = jnp.einsum("ckb,ba->cka", freq_re, cos_inner, precision=PRECISE_SETTING) - jnp.einsum(
        "ckb,ba->cka", freq_im, sin_inner, precision=PRECISE_SETTING
    )
    mid_im = jnp.einsum("ckb,ba->cka", freq_im, cos_inner, precision=PRECISE_SETTING) + jnp.einsum(
        "ckb,ba->cka", freq_re, sin_inner, precision=PRECISE_SETTING
    )
    rotated_real = mid_re * twist_cos[None] - mid_im * twist_sin[None]
    rotated_imaginary = mid_re * twist_sin[None] + mid_im * twist_cos[None]
    outcome = jnp.einsum(
        "bl,yls->ybs", outer_cosine[:outer_half_length], rotated_real, precision=PRECISE_SETTING
    ) - jnp.einsum(
        "bl,yls->ybs", outer_sine[:outer_half_length], rotated_imaginary, precision=PRECISE_SETTING
    )
    return outcome.reshape(freq_re.shape[0], outer_half_length * inner_len) / (
        outer_len * inner_len
    )


def pole_sum(rate_rows, residue_rows, seq_len):
    positions = jnp.arange(seq_len, dtype=jnp.float32)

    def add_pole(pole_index, running):
        return running + residue_rows[pole_index][:, None] * jnp.exp(
            -rate_rows[pole_index][:, None] * positions[None, :]
        )

    return lax.fori_loop(
        0, rate_rows.shape[0], add_pole, jnp.zeros((rate_rows.shape[1], seq_len), jnp.float32)
    )


def filter_float(product_rows, kernel_re, kernel_im, plan):
    signal_re, signal_im = forward_spectrum(product_rows, plan)
    joined_re = signal_re * kernel_re - signal_im * kernel_im
    joined_im = signal_re * kernel_im + signal_im * kernel_re
    return inverse_real(joined_re, joined_im, plan)


def filter_product(product_rows, kernel_re, kernel_im, plan):
    return filter_float(product_rows, kernel_re, kernel_im, plan).astype(jnp.bfloat16)


def channel_kernel(decay_rates, residues, first_channel, narrow, seq_len, plan):
    rate_rows = lax.dynamic_slice_in_dim(decay_rates, first_channel, narrow, 1)
    residue_rows = lax.dynamic_slice_in_dim(residues, first_channel, narrow, 1)
    return forward_spectrum(pole_sum(rate_rows, residue_rows, seq_len), plan)


def per_device(
    query_stream, key_stream, value_stream, conv_weight, decay_rates, residues, skip_gain
):
    tok_rows, local_width = query_stream.shape
    groups = lax.axis_size("ctx")
    narrow = local_width // groups
    seq_len = tok_rows * groups
    first_channel = lax.axis_index("ctx") * narrow
    plan = transform_plan(seq_len)
    kernel_re, kernel_im = channel_kernel(
        decay_rates, residues, first_channel, narrow, seq_len, plan
    )
    streams = jnp.stack([query_stream, key_stream, value_stream])
    arranged = jnp.transpose(streams, (0, 2, 1)).reshape(3, groups, narrow, tok_rows)
    whole_seq = lax.all_to_all(arranged, "ctx", split_axis=1, concat_axis=3, tiled=True)
    whole_seq = whole_seq.reshape(3, narrow, seq_len).astype(jnp.float32)
    tap_weights = lax.dynamic_slice_in_dim(conv_weight, first_channel, narrow, 2)
    padded = jnp.pad(whole_seq, ((0, 0), (0, 0), (2, 0)))
    shorts = (
        tap_weights[:, 0, :, None] * whole_seq
        + tap_weights[:, 1, :, None] * padded[:, :, 1:-1]
        + tap_weights[:, 2, :, None] * padded[:, :, :-2]
    )
    product = lax.optimization_barrier((shorts[1] * shorts[2]).astype(jnp.bfloat16))
    long_part = lax.optimization_barrier(
        filter_product(product.astype(jnp.float32), kernel_re, kernel_im, plan)
    )
    skip_rows = lax.dynamic_slice_in_dim(skip_gain, first_channel, narrow, 0)
    mixed_sum = long_part.astype(jnp.float32) + skip_rows[:, None] * product.astype(jnp.float32)
    result = (shorts[0] * mixed_sum).astype(jnp.bfloat16)
    returned = lax.all_to_all(
        result.reshape(1, narrow, seq_len), "ctx", split_axis=2, concat_axis=0, tiled=True
    )
    return returned.reshape(local_width, tok_rows).T


def solution(mesh):
    in_specs = (
        P("ctx", "fsdp"),
        P("ctx", "fsdp"),
        P("ctx", "fsdp"),
        P(None, None, "fsdp"),
        P(None, "fsdp"),
        P(None, "fsdp"),
        P("fsdp"),
    )
    out_specs = P("ctx", "fsdp")
    return jax.shard_map(
        per_device, mesh=mesh, in_specs=in_specs, out_specs=out_specs, check_vma=False
    )
```

profile of v0, /device:TPU:6, one launch (start us, length us, event | category | flops | bytes accessed | tf_op | source)
XLA Modules:
  0.0 208.6 jit_solution(16046938639940275945)
XLA Ops:
  0.0 1.0 copy.114
  1.0 1.0 copy.115
  2.1 1.0 copy.116
  4.0 32.0 %all-to-all-start = ((bf16[3,64,8,128]{3,2,0,1:T(8,128)(2,1)}), bf16[3,64,8,128]{3,2,0,1:T(8,128)(2,1)S(1)}, u32[]{:S(2)}, u32[]{:S(2)}) async-start(bf16[3,64,8,128]{3,2,0,1:T(8,128)(2,1)} %copy.117), calls=%async_computation | async-start | bytes 786432 | tf_op jit(solution)/shard_map/all_to_all | solution.py:123
  36.8 2.7 %while.14 = (s32[]{:T(128)}, f32[8,8192]{1,0:T(8,128)S(1)}, f32[16,8]{1,0:T(8,128)S(1)}, f32[16,8]{1,0:T(8,128)S(1)}, s32[]{:T(128)}, /*index=5*/s32[]{:T(128)}) while((s32[]{:T(128)}, f32[8,8192]{1,0:T(8,128)S(1)}, f32[16,8]{1,0:T(8,128)S(1)}, f32[16,8]{1,0:T(8,128)S(1)}, s32[]{:T(128)}, /*index=5*/s32[]{:T(128)}) %tuple.41), condition=%wide.region_1.2_spmd.clone, body=%wide.region_0.1_spmd.clone.sunk | while | flops 262155 | bytes 524571 | solution.py:87
  41.9 1.0 fusion.5
  42.9 1.0 convolution_bitcast_fusion
  43.9 1.2 fusion.33
  45.1 1.2 fusion.32
  46.3 1.2 convolution_subtract_fusion.1
  47.6 1.2 convolution_add_fusion.1
  48.8 35.3 %all-to-all-done = bf16[3,64,8,128]{3,2,0,1:T(8,128)(2,1)S(1)} async-done(((bf16[3,64,8,128]{3,2,0,1:T(8,128)(2,1)}), bf16[3,64,8,128]{3,2,0,1:T(8,128)(2,1)S(1)}, u32[]{:S(2)}, u32[]{:S(2)}) %all-to-all-start) | async-done | bytes 393248 | tf_op jit(solution)/shard_map/all_to_all | solution.py:123
  85.9 1.2 fusion.31
  87.1 1.2 fusion.30
  88.3 1.4 convolution_add_fusion.2
  89.6 1.2 multiply_subtract_fusion
  92.6 0.9 convolution_subtract_fusion
  93.5 0.9 convolution_add_fusion
  96.2 6.8 %copy.151 = bf16[1,8,8192]{1,0,2:T(2,128)(2,1)} copy(bf16[1,8,8192]{2,1,0:T(8,128)(2,1)S(1)} %fusion.26) | data formatting | bytes 262144 | tf_op jit(solution)/shard_map/reshape | solution.py:140
  103.4 45.4 %reduce = bf16[8192,8]{1,0:T(8,128)(2,1)S(1)} reduce(bf16[8192,1,8]{2,1,0:T(2,128)(2,1)} %bitcast.129, bf16[]{:T(256)} %broadcast.171), dimensions={1}, to_apply=%bitcast.114.reduce_sub_computation | reduce | bytes 262146
  148.9 2.3 %reshape.103 = bf16[64,2,512]{2,1,0:T(2,128)(2,1)S(1)} reshape(bf16[8192,8]{1,0:T(8,128)(2,1)S(1)} %reduce) | data formatting | bytes 262144
  151.2 40.0 %all_to_all.24 = bf16[64,2,512]{2,1,0:T(2,128)(2,1)S(1)} all-to-all(bf16[64,2,512]{2,1,0:T(2,128)(2,1)S(1)} %reshape.103), channel_id=1, replica_groups=mesh['ctx'=64,'fsdp'=16] {'ctx'}, dimensions={0} | all-to-all | bytes 262144 | tf_op jit(solution)/shard_map/all_to_all | solution.py:139
  191.2 8.7 %reshape.104 = bf16[8192,1,8]{2,1,0:T(2,128)(2,1)} reshape(bf16[64,2,512]{2,1,0:T(2,128)(2,1)S(1)} %all_to_all.24) | data formatting | bytes 262144
  199.9 7.8 %copy.152 = bf16[1,8,8192]{2,1,0:T(8,128)(2,1)S(1)} copy(bf16[1,8,8192]{1,0,2:T(2,128)(2,1)} %bitcast.130) | data formatting | bytes 262144 | tf_op jit(solution)/shard_map/all_to_all | solution.py:139
  (60 shorter events, 12.9 us)
Async XLA Ops:
  4.0 80.1 %all-to-all-start = ((bf16[3,64,8,128]{3,2,0,1:T(8,128)(2,1)}), bf16[3,64,8,128]{3,2,0,1:T(8,128)(2,1)S(1)}, u32[]{:S(2)}, u32[]{:S(2)}) async-start(bf16[3,64,8,128]{3,2,0,1:T(8,128)(2,1)} %copy.117), calls=%async_computation | async-start | bytes 786432 | tf_op jit(solution)/shard_map/all_to_all | solution.py:123
where the time goes:
time: 212 us; the launch traced here: 209 us
  other arithmetic  49.2 us (23%)
  blocking collectives  40 us (19%)
  waiting for transfers between devices  35.3 us (17%)
  local copies, waits for them, and re-layouts  33.6 us (16%)
  starting transfers between devices  32 us (15%)
  matrix products  17.7 us (8%)
    unnamed x2, other arithmetic  45.4 us
    all_to_all x1, blocking collectives, per_device(): lax.all_to_all(result.reshape(1, narrow, seq_len), 'ctx', split_axis=2, c...  40 us
    all_to_all x1, waiting for transfers between devices, per_device(): lax.all_to_all(arranged, 'ctx', split_axis=1, concat_axis=3, tiled=True)  35.3 us
    all_to_all x1, starting transfers between devices, per_device(): lax.all_to_all(arranged, 'ctx', split_axis=1, concat_axis=3, tiled=True)  32 us
    unnamed x10, local copies, waits for them, and re-layouts  14.7 us
    all_to_all x2, local copies, waits for them, and re-layouts, per_device(): lax.all_to_all(result.reshape(1, narrow, seq_len), 'ctx', split_axis=2, c...  7.88 us
    reshape x1, local copies, waits for them, and re-layouts, per_device(): result.reshape(1, narrow, seq_len)  6.76 us
  transfers between devices with their start and end apart: 1, of which 1 were waited for; matrix products, arithmetic and copies ran while one was open for 6% of the time, Pallas kernels for 0%

commit v1 on v0

v1 whole, which is shorter than its diff:
```python
import functools

import jax
import jax.numpy as jnp
from jax import lax
from jax.experimental import pallas as pl
from jax.experimental.pallas import tpu as pltpu
from jax.sharding import PartitionSpec as P

MESH = pl.DeviceIdType.MESH
F32 = jnp.float32
BF16 = jnp.bfloat16
SUB = 16
PAD = 8
MEMBERS = 4
LANES = 128


def kernel(
    z_len, groups,
    q_hbm, k_hbm, v_hbm, cw_ref, rate_ref, res_ref, skip_ref, out_ref,
    raw, padded, edge, halo, xs, qs, etab, hpad, htab, ylocal, prefix, carried,
    apow, tbuf, got1, gbuf, got2, cbuf, got3,
    in_sem, halo_send, halo_recv, send1, recv1, sendx, recvx, send2, recv2, send3, recv3,
):
    tokens, width = out_ref.shape
    subs = tokens // SUB
    quarters = width // LANES
    poles = rate_ref.shape[0]
    ctx = lax.axis_index("ctx")
    half, z = ctx // z_len, ctx % z_len
    group, member = z // MEMBERS, z % MEMBERS
    ctx_len = 2 * z_len

    def place(to_half, to_group, to_member):
        return {"ctx": to_half * z_len + to_group * MEMBERS + to_member}

    loads = []
    for i, ref in enumerate((k_hbm, v_hbm, q_hbm)):
        load = pltpu.make_async_copy(ref, raw.at[i], in_sem.at[i])
        load.start()
        loads.append(load)

    after = {"ctx": lax.rem(ctx + 1, ctx_len)}
    before = {"ctx": lax.rem(ctx + ctx_len - 1, ctx_len)}
    partners = [after, before]
    for o in range(1, MEMBERS):
        partners.append(place(half, group, (member + o) % MEMBERS))
    for o in range(MEMBERS):
        partners.append(place(1 - half, group, o))
    for o in range(1, groups):
        partners.append(place(half, (group + o) % groups, member))
    barrier = pltpu.get_barrier_semaphore()
    for partner in partners:
        pl.semaphore_signal(barrier, inc=1, device_id=partner, device_id_type=MESH)

    steps = lax.broadcasted_iota(jnp.int32, (SUB, width), 0).astype(F32)
    taps = jnp.zeros((SUB, width), F32)
    for n in range(poles):
        row = res_ref[n : n + 1, :] * jnp.exp(-rate_ref[n : n + 1, :] * steps)
        etab[n] = row
        taps = taps + row
    hpad[0:SUB, :] = jnp.zeros((SUB, width), F32)
    hpad[SUB:, :] = taps
    for l in range(quarters):
        rates = rate_ref[:, l * LANES : (l + 1) * LANES]
        for i, power in enumerate((1, 2, 3) + tuple(range(4, 4 * groups + 1, 4))):
            apow[i, l] = jnp.exp(-rates * float(power * tokens))

    for i in range(3):
        loads[i].wait()
        padded[i, PAD:, :] = raw[i].astype(F32)
        edge[2 * i : 2 * i + 2, :] = padded[i, PAD + tokens - 2 :, :]
    edge[6:8, :] = jnp.zeros((2, width), F32)

    pl.semaphore_wait(barrier, len(partners))
    halo_copy = pltpu.make_async_remote_copy(
        edge, halo, halo_send, halo_recv, device_id=after, device_id_type=MESH
    )
    halo_copy.start()

    def short(i, stream, lo, hi):
        return (
            cw_ref[stream, 0:1, :] * padded[i, PAD + lo : PAD + hi, :]
            + cw_ref[stream, 1:2, :] * padded[i, PAD + lo - 1 : PAD + hi - 1, :]
            + cw_ref[stream, 2:3, :] * padded[i, PAD + lo - 2 : PAD + hi - 2, :]
        )

    def filter_rows(lo, hi):
        product = short(0, 1, lo, hi) * short(1, 2, lo, hi)
        xs[lo:hi, :] = product.astype(BF16).astype(F32)
        qs[lo:hi, :] = short(2, 0, lo, hi)

    def inner_states(blocks):
        for l in range(quarters):
            lanes = slice(l * LANES, (l + 1) * LANES)
            decay = jnp.exp(-rate_ref[:, lanes])
            states = [jnp.zeros((poles, LANES), F32) for _ in blocks]
            for s in range(SUB):
                for i, b in enumerate(blocks):
                    t = b * SUB + s
                    states[i] = (states[i] + xs[t : t + 1, lanes]) * decay
            for i, b in enumerate(blocks):
                prefix[b, l] = states[i]

    for b in range(1, subs):
        filter_rows(b * SUB, (b + 1) * SUB)
    inner_states(range(1, subs))
    halo_copy.wait()
    for i in range(3):
        padded[i, PAD - 2 : PAD, :] = jnp.where(ctx > 0, halo[2 * i : 2 * i + 2, :], 0.0)
    filter_rows(0, SUB)
    inner_states([0])

    for l in range(quarters):
        decay = jnp.exp(-rate_ref[:, l * LANES : (l + 1) * LANES] * float(SUB))
        state = jnp.zeros((poles, LANES), F32)
        for b in range(subs):
            grown = prefix[b, l]
            prefix[b, l] = state
            state = state * decay + grown
        tbuf[l] = state

    copies1 = []
    for o in range(1, MEMBERS):
        to = (member + o) % MEMBERS
        copy = pltpu.make_async_remote_copy(
            tbuf.at[to], got1.at[1, member], send1.at[o], recv1.at[member],
            device_id=place(half, group, to), device_id_type=MESH,
        )
        copy.start()
        copies1.append(copy)

    @pl.when(half == 0)
    def _():
        for o in range(MEMBERS):
            pltpu.make_async_remote_copy(
                tbuf.at[o], got1.at[0, member], sendx.at[o], recvx.at[member],
                device_id=place(1, group, o), device_id_type=MESH,
            ).start()

    for s in range(SUB):
        htab[s] = hpad[SUB - s : 2 * SUB - s, :]

    got1[1, member] = tbuf[member]
    for o in range(1, MEMBERS):
        source = (member + o) % MEMBERS
        pltpu.make_async_remote_copy(
            tbuf.at[0], got1.at[1, source], send1.at[o], recv1.at[source],
            device_id=place(half, group, source), device_id_type=MESH,
        ).wait_recv()

    @pl.when(half == 1)
    def _():
        for o in range(MEMBERS):
            pltpu.make_async_remote_copy(
                tbuf.at[0], got1.at[0, o], sendx.at[o], recvx.at[o],
                device_id=place(0, group, o), device_id_type=MESH,
            ).wait_recv()

    @pl.when(half == 0)
    def _():
        for o in range(MEMBERS):
            got1[0, o] = jnp.zeros((poles, LANES), F32)

    def total(side):
        return (
            got1[side, 3] + apow[0, member] * got1[side, 2]
            + apow[1, member] * got1[side, 1] + apow[2, member] * got1[side, 0]
        )

    first_total = total(0)
    own_total = total(1)
    gbuf[0] = own_total + apow[2 + groups, member] * first_total
    gbuf[1] = first_total

    copies2 = []
    for o in sorted(range(1, groups), key=lambda o: -min(o, groups - o)):
        wraps = (group + o) // groups
        copy = pltpu.make_async_remote_copy(
            gbuf.at[wraps], got2.at[o], send2.at[o], recv2.at[o],
            device_id=place(half, (group + o) % groups, member), device_id_type=MESH,
        )
        copy.start()
        copies2.append(copy)

    for l in range(quarters):
        lanes = slice(l * LANES, (l + 1) * LANES)
        sums = [jnp.zeros((SUB, LANES), F32) for _ in range(subs)]
        for s in range(SUB):
            table = htab[s, :, lanes]
            for b in range(subs):
                t = b * SUB + s
                sums[b] = sums[b] + table * xs[t : t + 1, lanes]
        for n in range(poles):
            table = etab[n, :, lanes]
            for b in range(1, subs):
                sums[b] = sums[b] + table * prefix[b, l, n : n + 1, :]
        for b in range(subs):
            ylocal[b * SUB : (b + 1) * SUB, lanes] = sums[b]

    inside = got1[1, 0]
    inner = [jnp.zeros((poles, LANES), F32), inside]
    for o in range(1, MEMBERS - 1):
        inside = inside * apow[0, member] + got1[1, o]
        inner.append(inside)
    carry = apow[2 + groups - 1, member] * gbuf[1]
    for o in sorted(range(1, groups), key=lambda o: min(o, groups - o)):
        pltpu.make_async_remote_copy(
            gbuf.at[0], got2.at[o], send2.at[o], recv2.at[o],
            device_id=place(half, (group + o) % groups, member), device_id_type=MESH,
        ).wait_recv()
        carry = carry + (got2[o] if o == 1 else apow[2 + o - 1, member] * got2[o])
    cbuf[0] = carry
    for o in range(1, MEMBERS):
        cbuf[o] = apow[o - 1, member] * carry + inner[o]
    got3[member] = cbuf[member]
    for o in range(1, MEMBERS):
        to = (member + o) % MEMBERS
        pltpu.make_async_remote_copy(
            cbuf.at[to], got3.at[member], send3.at[o], recv3.at[member],
            device_id=place(half, group, to), device_id_type=MESH,
        ).start()
    for o in range(1, MEMBERS):
        source = (member + o) % MEMBERS
        pltpu.make_async_remote_copy(
            cbuf.at[0], got3.at[source], send3.at[o], recv3.at[source],
            device_id=place(half, group, source), device_id_type=MESH,
        ).wait_recv()

    for l in range(quarters):
        lanes = slice(l * LANES, (l + 1) * LANES)
        decay = jnp.exp(-rate_ref[:, lanes] * float(SUB))
        state = got3[l]
        for b in range(subs):
            carried[b, l] = state
            state = state * decay
        sums = [ylocal[b * SUB : (b + 1) * SUB, lanes] for b in range(subs)]
        for n in range(poles):
            table = etab[n, :, lanes]
            for b in range(subs):
                sums[b] = sums[b] + table * carried[b, l, n : n + 1, :]
        for b in range(subs):
            rows = slice(b * SUB, (b + 1) * SUB)
            mixed = sums[b].astype(BF16).astype(F32) + skip_ref[:, lanes] * xs[rows, lanes]
            out_ref[rows, lanes] = (qs[rows, lanes] * mixed).astype(BF16)

    for copy in copies1 + copies2:
        copy.wait_send()

    @pl.when(half == 0)
    def _():
        for o in range(MEMBERS):
            pltpu.make_async_remote_copy(
                tbuf.at[o], got1.at[0, member], sendx.at[o], recvx.at[member],
                device_id=place(1, group, o), device_id_type=MESH,
            ).wait_send()

    for o in range(1, MEMBERS):
        to = (member + o) % MEMBERS
        pltpu.make_async_remote_copy(
            cbuf.at[to], got3.at[member], send3.at[o], recv3.at[member],
            device_id=place(half, group, to), device_id_type=MESH,
        ).wait_send()


def per_device(
    query_stream, key_stream, value_stream, conv_weight, decay_rates, residues, skip_gain
):
    tokens, width = query_stream.shape
    poles = decay_rates.shape[0]
    z_len = lax.axis_size("ctx") // 2
    groups = z_len // MEMBERS
    quarters = width // LANES
    subs = tokens // SUB
    vmem = pltpu.VMEM
    state = (poles, LANES)
    dma = pltpu.SemaphoreType.DMA
    whole = pl.BlockSpec(memory_space=pltpu.VMEM)
    anywhere = pl.BlockSpec(memory_space=pl.ANY)
    return pl.pallas_call(
        functools.partial(kernel, z_len, groups),
        out_shape=jax.ShapeDtypeStruct((tokens, width), BF16),
        in_specs=[anywhere] * 3 + [whole] * 4,
        out_specs=whole,
        scratch_shapes=[
            vmem((3, tokens, width), BF16),
            vmem((3, PAD + tokens, width), F32),
            vmem((8, width), F32),
            vmem((8, width), F32),
            vmem((tokens, width), F32),
            vmem((tokens, width), F32),
            vmem((poles, SUB, width), F32),
            vmem((2 * SUB, width), F32),
            vmem((SUB, SUB, width), F32),
            vmem((tokens, width), F32),
            vmem((subs, quarters) + state, F32),
            vmem((subs, quarters) + state, F32),
            vmem((3 + groups, quarters) + state, F32),
            vmem((quarters,) + state, F32),
            vmem((2, MEMBERS) + state, F32),
            vmem((2,) + state, F32),
            vmem((groups,) + state, F32),
            vmem((MEMBERS,) + state, F32),
            vmem((quarters,) + state, F32),
            dma((3,)), dma, dma,
            dma((MEMBERS,)), dma((MEMBERS,)), dma((MEMBERS,)), dma((MEMBERS,)),
            dma((groups,)), dma((groups,)), dma((MEMBERS,)), dma((MEMBERS,)),
        ],
        compiler_params=pltpu.CompilerParams(
            collective_id=0, has_side_effects=True, vmem_limit_bytes=40 * 1024 * 1024
        ),
        name="modal_scan",
    )(query_stream, key_stream, value_stream, conv_weight, decay_rates, residues,
      skip_gain.reshape(1, width))


def solution(mesh):
    in_specs = (
        P("ctx", "fsdp"),
        P("ctx", "fsdp"),
        P("ctx", "fsdp"),
        P(None, None, "fsdp"),
        P(None, "fsdp"),
        P(None, "fsdp"),
        P("fsdp"),
    )
    return jax.shard_map(
        per_device, mesh=mesh, in_specs=in_specs, out_specs=P("ctx", "fsdp"), check_vma=False
    )
```

time: 212 us -> 58.2 us (0.27); the launches traced: 209 us -> 57.8 us
  Pallas kernels: 0 us -> 51.5 us
  other arithmetic: 49.2 us -> 0 us
  blocking collectives: 40 us -> 0 us
  waiting for transfers between devices: 35.3 us -> 0 us
  starting transfers between devices: 32 us -> 0 us
  local copies, waits for them, and re-layouts: 33.6 us -> 6.3 us
  matrix products: 17.7 us -> 0 us
    pallas_call x0 -> x1, Pallas kernels: none -> 51.5 us  [per_device(): pl.pallas_call(functools.partial(kernel, z_len, groups), out_shape=jax.Sh...]
    unnamed x2 -> x0, other arithmetic: 45.4 us -> none
    all_to_all x1 -> x0, blocking collectives: 40 us -> none  [per_device(): lax.all_to_all(result.reshape(1, narrow, seq_len), 'ctx', split_axis=2, c...]
    all_to_all x1 -> x0, waiting for transfers between devices: 35.3 us -> none  [per_device(): lax.all_to_all(arranged, 'ctx', split_axis=1, concat_axis=3, tiled=True)]
    all_to_all x1 -> x0, starting transfers between devices: 32 us -> none  [per_device(): lax.all_to_all(arranged, 'ctx', split_axis=1, concat_axis=3, tiled=True)]
    dot_general x18 -> x0, matrix products: 17.7 us -> none  [the longest x2 2.58 us: forward_spectrum(): jnp.einsum('cka,ab->ckb', twist_im, sin_inner, precision=PRECISE_SETTING)]
    unnamed x10 -> x15, local copies, waits for them, and re-layouts: 14.7 us -> 6.3 us
    all_to_all x2 -> x0, local copies, waits for them, and re-layouts: 7.88 us -> none  [per_device(): lax.all_to_all(result.reshape(1, narrow, seq_len), 'ctx', split_axis=2, c...]
  transfers between devices with their start and end apart: 1 -> 0, of which waited for: 1 -> 0; matrix products, arithmetic and copies ran while one was open for 6% -> 0% of each run, Pallas kernels for 0% -> 0%
where the time goes in v1:
time: 58.2 us; the launch traced here: 57.8 us
  Pallas kernels  51.5 us (88%)
  local copies, waits for them, and re-layouts  6.3 us (11%)
    pallas_call x1, Pallas kernels, per_device(): pl.pallas_call(functools.partial(kernel, z_len, groups), out_shape=jax.Sh...  51.5 us
    unnamed x15, local copies, waits for them, and re-layouts  6.3 us

profile of v1, /device:TPU:6, one launch (start us, length us, event | category | flops | bytes accessed | tf_op | source)
XLA Modules:
  0.0 57.8 jit_solution(9503104783958140589)
XLA Ops:
  0.0 0.0 copy-start
  0.0 0.9 %copy-done = bf16[128,512]{1,0:T(8,128)(2,1)S(1)} copy-done((bf16[128,512]{1,0:T(8,128)(2,1)S(1)}, bf16[128,512]{1,0:T(8,128)(2,1)}, u32[]{:S(2)}) %copy-start) | copy-done | bytes 131096
  0.9 0.0 copy-start.1
  0.9 0.9 %copy-done.1 = bf16[128,512]{1,0:T(8,128)(2,1)S(1)} copy-done((bf16[128,512]{1,0:T(8,128)(2,1)S(1)}, bf16[128,512]{1,0:T(8,128)(2,1)}, u32[]{:S(2)}) %copy-start.1) | copy-done | bytes 131096
  1.8 0.0 copy-start.2
  1.8 0.9 %copy-done.2 = bf16[128,512]{1,0:T(8,128)(2,1)S(1)} copy-done((bf16[128,512]{1,0:T(8,128)(2,1)S(1)}, bf16[128,512]{1,0:T(8,128)(2,1)}, u32[]{:S(2)}) %copy-start.2) | copy-done | bytes 131096
  2.7 0.0 copy-start.3
  2.7 0.8 %copy-done.3 = f32[16,512]{1,0:T(8,128)S(1)} copy-done((f32[16,512]{1,0:T(8,128)S(1)}, f32[16,512]{1,0:T(8,128)}, u32[]{:S(2)}) %copy-start.3) | copy-done | bytes 32792
  3.5 0.0 copy-start.4
  3.5 0.8 %copy-done.4 = f32[16,512]{1,0:T(8,128)S(1)} copy-done((f32[16,512]{1,0:T(8,128)S(1)}, f32[16,512]{1,0:T(8,128)}, u32[]{:S(2)}) %copy-start.4) | copy-done | bytes 32792
  4.2 0.0 copy-start.5
  4.2 0.7 %copy-done.5 = f32[3,3,512]{2,1,0:T(4,128)S(1)} copy-done((f32[3,3,512]{2,1,0:T(4,128)S(1)}, f32[3,3,512]{2,1,0:T(4,128)}, u32[]{:S(2)}) %copy-start.5) | copy-done | bytes 18456
  5.0 0.0 copy-start.6
  5.0 0.7 %copy-done.6 = f32[512]{0:T(512)S(1)} copy-done((f32[512]{0:T(512)S(1)}, f32[512]{0:T(512)}, u32[]{:S(2)}) %copy-start.6) | copy-done | bytes 2072
  5.7 51.5 %modal_scan.1 = bf16[128,512]{1,0:T(8,128)(2,1)S(1)} custom-call(bf16[128,512]{1,0:T(8,128)(2,1)S(1)} %copy-done, bf16[128,512]{1,0:T(8,128)(2,1)S(1)} %copy-done.1, bf16[128,512]{1,0:T(8,128)(2,1)S(1)} %copy-done.2, f32[3,3,512]{2,1,0:T(4,128)S(1)} %copy-done.5, f32[16,512]{1,0:T(8,128)S(1)} %copy-done.3, f32[16,512]{1,0:T(8,128)S(1)} %copy-done.4, ...), custom_call_target="tpu_custom_call" | custom-call | tf_op jit(solution)/shard_map/modal_scan/pallas_call | solution.py:281
  57.1 0.7 %copy.9 = bf16[128,512]{1,0:T(8,128)(2,1)} copy(bf16[128,512]{1,0:T(8,128)(2,1)S(1)} %modal_scan.1) | data formatting | bytes 262144
Async XLA Ops:
  0.0 0.9 %copy-start = (bf16[128,512]{1,0:T(8,128)(2,1)S(1)}, bf16[128,512]{1,0:T(8,128)(2,1)}, u32[]{:S(2)}) copy-start(bf16[128,512]{1,0:T(8,128)(2,1)} %q_hbm.1) | copy-start | bytes 393220
  0.9 0.9 %copy-start.1 = (bf16[128,512]{1,0:T(8,128)(2,1)S(1)}, bf16[128,512]{1,0:T(8,128)(2,1)}, u32[]{:S(2)}) copy-start(bf16[128,512]{1,0:T(8,128)(2,1)} %k_hbm.1) | copy-start | bytes 393220
  1.8 0.9 %copy-start.2 = (bf16[128,512]{1,0:T(8,128)(2,1)S(1)}, bf16[128,512]{1,0:T(8,128)(2,1)}, u32[]{:S(2)}) copy-start(bf16[128,512]{1,0:T(8,128)(2,1)} %v_hbm.1) | copy-start | bytes 393220
  2.7 0.8 %copy-start.3 = (f32[16,512]{1,0:T(8,128)S(1)}, f32[16,512]{1,0:T(8,128)}, u32[]{:S(2)}) copy-start(f32[16,512]{1,0:T(8,128)} %rate_ref.1) | copy-start | bytes 98308
  3.5 0.8 %copy-start.4 = (f32[16,512]{1,0:T(8,128)S(1)}, f32[16,512]{1,0:T(8,128)}, u32[]{:S(2)}) copy-start(f32[16,512]{1,0:T(8,128)} %res_ref.1) | copy-start | bytes 98308
  4.2 0.7 %copy-start.5 = (f32[3,3,512]{2,1,0:T(4,128)S(1)}, f32[3,3,512]{2,1,0:T(4,128)}, u32[]{:S(2)}) copy-start(f32[3,3,512]{2,1,0:T(4,128)} %cw_ref.1) | copy-start | bytes 55300
  5.0 0.7 %copy-start.6 = (f32[512]{0:T(512)S(1)}, f32[512]{0:T(512)}, u32[]{:S(2)}) copy-start(f32[512]{0:T(512)} %param.13) | copy-start | bytes 6148

commit v2 on v1

--- a/solution.py
+++ b/solution.py
@@ -18,10 +18,10 @@
 
 def kernel(
     z_len, groups,
-    q_hbm, k_hbm, v_hbm, cw_ref, rate_ref, res_ref, skip_ref, out_ref,
-    raw, padded, edge, halo, xs, qs, etab, hpad, htab, ylocal, prefix, carried,
+    q_hbm, k_hbm, v_hbm, cw_hbm, rate_hbm, res_hbm, skip_hbm, out_ref,
+    cw_ref, rate_ref, res_ref, skip_ref, raw, padded, edge, halo, xs, qs, etab, hpad, htab, ylocal, prefix, carried,
     apow, tbuf, got1, gbuf, got2, cbuf, got3,
-    in_sem, halo_send, halo_recv, send1, recv1, sendx, recvx, send2, recv2, send3, recv3,
+    in_sem, known, halo_send, halo_recv, send1, recv1, sendx, recvx, send2, recv2, send3, recv3,
 ):
     tokens, width = out_ref.shape
     subs = tokens // SUB
@@ -36,23 +36,35 @@
         return {"ctx": to_half * z_len + to_group * MEMBERS + to_member}
 
     loads = []
-    for i, ref in enumerate((k_hbm, v_hbm, q_hbm)):
-        load = pltpu.make_async_copy(ref, raw.at[i], in_sem.at[i])
+    for source, target in (
+        (rate_hbm, rate_ref), (res_hbm, res_ref), (k_hbm, raw.at[0]), (v_hbm, raw.at[1]),
+        (cw_hbm, cw_ref), (q_hbm, raw.at[2]), (skip_hbm, skip_ref),
+    ):
+        load = pltpu.make_async_copy(source, target, in_sem.at[len(loads)])
         load.start()
         loads.append(load)
 
     after = {"ctx": lax.rem(ctx + 1, ctx_len)}
     before = {"ctx": lax.rem(ctx + ctx_len - 1, ctx_len)}
-    partners = [after, before]
+    near = (1, 2, groups - 2, groups - 1)
+    partners = [before]
     for o in range(1, MEMBERS):
         partners.append(place(half, group, (member + o) % MEMBERS))
-    for o in range(MEMBERS):
-        partners.append(place(1 - half, group, o))
-    for o in range(1, groups):
+    for o in near:
         partners.append(place(half, (group + o) % groups, member))
     barrier = pltpu.get_barrier_semaphore()
     for partner in partners:
         pl.semaphore_signal(barrier, inc=1, device_id=partner, device_id_type=MESH)
+
+    @pl.when(half == 1)
+    def _():
+        for o in range(MEMBERS):
+            pl.semaphore_signal(
+                barrier, inc=1, device_id=place(0, group, o), device_id_type=MESH
+            )
+
+    loads[0].wait()
+    loads[1].wait()
 
     steps = lax.broadcasted_iota(jnp.int32, (SUB, width), 0).astype(F32)
     taps = jnp.zeros((SUB, width), F32)
@@ -67,13 +79,19 @@
         for i, power in enumerate((1, 2, 3) + tuple(range(4, 4 * groups + 1, 4))):
             apow[i, l] = jnp.exp(-rates * float(power * tokens))
 
+    for load in loads[2:]:
+        load.wait()
     for i in range(3):
-        loads[i].wait()
         padded[i, PAD:, :] = raw[i].astype(F32)
         edge[2 * i : 2 * i + 2, :] = padded[i, PAD + tokens - 2 :, :]
     edge[6:8, :] = jnp.zeros((2, width), F32)
 
-    pl.semaphore_wait(barrier, len(partners))
+    pl.semaphore_wait(barrier, len(partners) + MEMBERS * (1 - half))
+    for o in (2, groups - 2):
+        pl.semaphore_signal(
+            known, inc=1, device_id=place(half, (group + o) % groups, member),
+            device_id_type=MESH,
+        )
     halo_copy = pltpu.make_async_remote_copy(
         edge, halo, halo_send, halo_recv, device_id=after, device_id_type=MESH
     )
@@ -174,6 +192,7 @@
     gbuf[0] = own_total + apow[2 + groups, member] * first_total
     gbuf[1] = first_total
 
+    pl.semaphore_wait(known, 2)
     copies2 = []
     for o in sorted(range(1, groups), key=lambda o: -min(o, groups - o)):
         wraps = (group + o) // groups
@@ -277,13 +296,17 @@
     state = (poles, LANES)
     dma = pltpu.SemaphoreType.DMA
     whole = pl.BlockSpec(memory_space=pltpu.VMEM)
-    anywhere = pl.BlockSpec(memory_space=pl.ANY)
+    outside = pl.BlockSpec(memory_space=pltpu.HBM)
     return pl.pallas_call(
         functools.partial(kernel, z_len, groups),
         out_shape=jax.ShapeDtypeStruct((tokens, width), BF16),
-        in_specs=[anywhere] * 3 + [whole] * 4,
+        in_specs=[outside] * 7,
         out_specs=whole,
         scratch_shapes=[
+            vmem((3, 3, width), F32),
+            vmem((poles, width), F32),
+            vmem((poles, width), F32),
+            vmem((1, width), F32),
             vmem((3, tokens, width), BF16),
             vmem((3, PAD + tokens, width), F32),
             vmem((8, width), F32),
@@ -303,12 +326,12 @@
             vmem((groups,) + state, F32),
             vmem((MEMBERS,) + state, F32),
             vmem((quarters,) + state, F32),
-            dma((3,)), dma, dma,
+            dma((7,)), pltpu.SemaphoreType.REGULAR, dma, dma,
             dma((MEMBERS,)), dma((MEMBERS,)), dma((MEMBERS,)), dma((MEMBERS,)),
             dma((groups,)), dma((groups,)), dma((MEMBERS,)), dma((MEMBERS,)),
         ],
         compiler_params=pltpu.CompilerParams(
-            collective_id=0, has_side_effects=True, vmem_limit_bytes=40 * 1024 * 1024
+            collective_id=0, has_side_effects=True, vmem_limit_bytes=67_043_328
         ),
         name="modal_scan",
     )(query_stream, key_stream, value_stream, conv_weight, decay_rates, residues,

time: 58.2 us -> 49.6 us (0.85)
  local copies, waits for them, and re-layouts: 6.3 us -> 1.57 us
  Pallas kernels: 51.5 us -> 47.9 us
    unnamed x15 -> x1, local copies, waits for them, and re-layouts: 6.3 us -> 1.57 us
    pallas_call x1, Pallas kernels: 51.5 us -> 47.9 us  [per_device(): pl.pallas_call(functools.partial(kernel, z_len, groups), out_shape=jax.Sh...]
where the time goes in v2:
time: 49.6 us; the launch traced here: 49.4 us
  Pallas kernels  47.9 us (97%)
  local copies, waits for them, and re-layouts  1.57 us (3%)
    pallas_call x1, Pallas kernels, per_device(): pl.pallas_call(functools.partial(kernel, z_len, groups), out_shape=jax.Sh...  47.9 us
    unnamed x1, local copies, waits for them, and re-layouts  1.57 us

profile of v2, /device:TPU:6, one launch (start us, length us, event | category | flops | bytes accessed | tf_op | source)
XLA Modules:
  0.0 49.4 jit_solution(16170030584205514632)
XLA Ops:
  0.0 47.9 %modal_scan.1 = bf16[128,512]{1,0:T(8,128)(2,1)} custom-call(bf16[128,512]{1,0:T(8,128)(2,1)} %q_hbm.1, bf16[128,512]{1,0:T(8,128)(2,1)} %k_hbm.1, bf16[128,512]{1,0:T(8,128)(2,1)} %v_hbm.1, f32[3,3,512]{2,1,0:T(4,128)} %cw_hbm.1, f32[16,512]{1,0:T(8,128)} %rate_hbm.1, f32[16,512]{1,0:T(8,128)} %res_hbm.1, f32[1,512]{1,0:T(1,128)} %bitcast.1), custom_call_target="tpu_custom_call" | custom-call | tf_op jit(solution)/shard_map/modal_scan/pallas_call | solution.py:300
  47.9 1.6 %copy.9 = bf16[128,512]{1,0:T(8,128)(2,1)} copy(bf16[128,512]{1,0:T(8,128)(2,1)} %modal_scan.1) | data formatting | bytes 262144

commit v3 on v2

--- a/solution.py
+++ b/solution.py
@@ -12,6 +12,7 @@
 BF16 = jnp.bfloat16
 SUB = 16
 PAD = 8
+EDGE = 8
 MEMBERS = 4
 LANES = 128
 
@@ -20,8 +21,8 @@
     z_len, groups,
     q_hbm, k_hbm, v_hbm, cw_hbm, rate_hbm, res_hbm, skip_hbm, out_ref,
     cw_ref, rate_ref, res_ref, skip_ref, raw, padded, edge, halo, xs, qs, etab, hpad, htab, ylocal, prefix, carried,
-    apow, tbuf, got1, gbuf, got2, cbuf, got3,
-    in_sem, known, halo_send, halo_recv, send1, recv1, sendx, recvx, send2, recv2, send3, recv3,
+    apow, taps_ref, dec_ref, tbuf, got1, prev, gbuf, got2, cbuf, got3,
+    in_sem, known, halo_send, halo_recv, send1, recv1, sendx, recvx, sende, recve, sendf, recvf, send2, recv2, send3, recv3,
 ):
     tokens, width = out_ref.shape
     subs = tokens // SUB
@@ -63,39 +64,29 @@
                 barrier, inc=1, device_id=place(0, group, o), device_id_type=MESH
             )
 
-    loads[0].wait()
-    loads[1].wait()
-
-    steps = lax.broadcasted_iota(jnp.int32, (SUB, width), 0).astype(F32)
-    taps = jnp.zeros((SUB, width), F32)
-    for n in range(poles):
-        row = res_ref[n : n + 1, :] * jnp.exp(-rate_ref[n : n + 1, :] * steps)
-        etab[n] = row
-        taps = taps + row
-    hpad[0:SUB, :] = jnp.zeros((SUB, width), F32)
-    hpad[SUB:, :] = taps
-    for l in range(quarters):
-        rates = rate_ref[:, l * LANES : (l + 1) * LANES]
-        for i, power in enumerate((1, 2, 3) + tuple(range(4, 4 * groups + 1, 4))):
-            apow[i, l] = jnp.exp(-rates * float(power * tokens))
-
-    for load in loads[2:]:
+    last = member == MEMBERS - 1
+    block = half * groups + group
+    left, right = lax.rem(block + 2 * groups - 1, 2 * groups), lax.rem(block + 1, 2 * groups)
+
+    @pl.when(block > 0)
+    def _():
+        pl.semaphore_signal(
+            barrier, inc=1, device_id=place(left // groups, left % groups, MEMBERS - 1),
+            device_id_type=MESH,
+        )
+
+    @pl.when((half == 1) & (group > 0))
+    def _():
+        pl.semaphore_signal(
+            barrier, inc=1, device_id=place(0, left % groups, MEMBERS - 1),
+            device_id_type=MESH,
+        )
+
+    for load in loads:
         load.wait()
-    for i in range(3):
+    for i in range(2):
+        padded[i, 0:PAD, :] = jnp.zeros((PAD, width), F32)
         padded[i, PAD:, :] = raw[i].astype(F32)
-        edge[2 * i : 2 * i + 2, :] = padded[i, PAD + tokens - 2 :, :]
-    edge[6:8, :] = jnp.zeros((2, width), F32)
-
-    pl.semaphore_wait(barrier, len(partners) + MEMBERS * (1 - half))
-    for o in (2, groups - 2):
-        pl.semaphore_signal(
-            known, inc=1, device_id=place(half, (group + o) % groups, member),
-            device_id_type=MESH,
-        )
-    halo_copy = pltpu.make_async_remote_copy(
-        edge, halo, halo_send, halo_recv, device_id=after, device_id_type=MESH
-    )
-    halo_copy.start()
 
     def short(i, stream, lo, hi):
         return (
@@ -104,10 +95,9 @@
             + cw_ref[stream, 2:3, :] * padded[i, PAD + lo - 2 : PAD + hi - 2, :]
         )
 
-    def filter_rows(lo, hi):
+    def products(lo, hi):
         product = short(0, 1, lo, hi) * short(1, 2, lo, hi)
         xs[lo:hi, :] = product.astype(BF16).astype(F32)
-        qs[lo:hi, :] = short(2, 0, lo, hi)
 
     def inner_states(blocks):
         for l in range(quarters):
@@ -121,23 +111,34 @@
             for i, b in enumerate(blocks):
                 prefix[b, l] = states[i]
 
-    for b in range(1, subs):
-        filter_rows(b * SUB, (b + 1) * SUB)
-    inner_states(range(1, subs))
-    halo_copy.wait()
-    for i in range(3):
-        padded[i, PAD - 2 : PAD, :] = jnp.where(ctx > 0, halo[2 * i : 2 * i + 2, :], 0.0)
-    filter_rows(0, SUB)
-    inner_states([0])
-
+    for b in range(subs):
+        products(b * SUB, (b + 1) * SUB)
+    xs[0:2, :] = jnp.zeros((2, width), F32)
+    for l in range(quarters):
+        lanes = slice(l * LANES, (l + 1) * LANES)
+        for i in range(2):
+            first = cw_ref[i + 1, 0:1, lanes] * padded[i, PAD : PAD + 2, lanes]
+            tbuf[l, poles + 2 * i : poles + 2 * i + 2, :] = first
+            second = cw_ref[i + 1, 1:2, lanes] * padded[i, PAD : PAD + 1, lanes]
+            tbuf[l, poles + 2 * i + 1 : poles + 2 * i + 2, :] = first[1:2, :] + second
+            tbuf[l, poles + 4 + 2 * i : poles + 6 + 2 * i, :] = padded[
+                i, PAD + tokens - 2 : PAD + tokens, lanes
+            ]
+    inner_states(range(subs))
     for l in range(quarters):
         decay = jnp.exp(-rate_ref[:, l * LANES : (l + 1) * LANES] * float(SUB))
-        state = jnp.zeros((poles, LANES), F32)
-        for b in range(subs):
-            grown = prefix[b, l]
-            prefix[b, l] = state
-            state = state * decay + grown
-        tbuf[l] = state
+        dec_ref[l] = decay
+        state = prefix[0, l]
+        for b in range(1, subs):
+            state = state * decay + prefix[b, l]
+        tbuf[l, 0:poles, :] = state
+
+    onward = MEMBERS * jnp.where(block < 2 * groups - 1, 1, 0)
+    across = MEMBERS * jnp.where((half == 0) & (group < groups - 1), 1, 0)
+    pl.semaphore_wait(
+        barrier,
+        MEMBERS + len(near) + MEMBERS * (1 - half) + jnp.where(last, onward + across, 0),
+    )
 
     copies1 = []
     for o in range(1, MEMBERS):
@@ -157,6 +158,56 @@
                 device_id=place(1, group, o), device_id_type=MESH,
             ).start()
 
+    edge_sends = []
+    for o in range(MEMBERS):
+        edge_sends.append((last & (block < 2 * groups - 1), pltpu.make_async_remote_copy(
+            tbuf.at[o, pl.ds(poles, EDGE)], prev.at[1], sende.at[o], recve,
+            device_id=place(right // groups, right % groups, o), device_id_type=MESH,
+        )))
+        edge_sends.append((last & (half == 0) & (group < groups - 1), pltpu.make_async_remote_copy(
+            tbuf.at[o, pl.ds(poles, EDGE)], prev.at[0], sendf.at[o], recvf,
+            device_id=place(1, right % groups, o), device_id_type=MESH,
+        )))
+    for due, copy in edge_sends:
+
+        @pl.when(due)
+        def _():
+            copy.start()
+
+    for o in (2, groups - 2):
+        pl.semaphore_signal(
+            known, inc=1, device_id=place(half, (group + o) % groups, member),
+            device_id_type=MESH,
+        )
+
+    padded[2, PAD:, :] = raw[2].astype(F32)
+    for i in range(3):
+        edge[2 * i : 2 * i + 2, :] = padded[i, PAD + tokens - 2 :, :]
+    edge[6:8, :] = jnp.zeros((2, width), F32)
+    halo_copy = pltpu.make_async_remote_copy(
+        edge, halo, halo_send, halo_recv, device_id=after, device_id_type=MESH
+    )
+    halo_copy.start()
+
+    steps = lax.broadcasted_iota(jnp.int32, (SUB, width), 0).astype(F32)
+    taps = jnp.zeros((SUB, width), F32)
+    for n in range(poles):
+        row = res_ref[n : n + 1, :] * jnp.exp(-rate_ref[n : n + 1, :] * steps)
+        etab[n] = row
+        taps = taps + row
+    hpad[0:SUB, :] = jnp.zeros((SUB, width), F32)
+    hpad[SUB:, :] = taps
+    for l in range(quarters):
+        rates = rate_ref[:, l * LANES : (l + 1) * LANES]
+        for i, power in enumerate((1, 2, 3) + tuple(range(4, 4 * groups + 1, 4))):
+            apow[i, l] = jnp.exp(-rates * float(power * tokens))
+
+    for l in range(quarters):
+        lanes = slice(l * LANES, (l + 1) * LANES)
+        rates = rate_ref[:, lanes]
+        apow[3 + groups, l] = jnp.exp(-rates * float(tokens - 1))
+        for i in range(2):
+            taps_ref[l, 2 * i : 2 * i + 2, :] = cw_ref[i + 1, 1:3, lanes]
     for s in range(SUB):
         htab[s] = hpad[SUB - s : 2 * SUB - s, :]
 
@@ -179,16 +230,59 @@
     @pl.when(half == 0)
     def _():
         for o in range(MEMBERS):
-            got1[0, o] = jnp.zeros((poles, LANES), F32)
-
-    def total(side):
+            got1[0, o] = jnp.zeros((poles + EDGE, LANES), F32)
+
+    @pl.when(block > 0)
+    def _():
+        pltpu.make_async_remote_copy(
+            tbuf.at[0, pl.ds(poles, EDGE)], prev.at[1], sende.at[0], recve,
+            device_id=after, device_id_type=MESH,
+        ).wait_recv()
+
+    @pl.when(block == 0)
+    def _():
+        prev[1] = jnp.zeros((EDGE, LANES), F32)
+
+    @pl.when((half == 1) & (group > 0))
+    def _():
+        pltpu.make_async_remote_copy(
+            tbuf.at[0, pl.ds(poles, EDGE)], prev.at[0], sendf.at[0], recvf,
+            device_id=after, device_id_type=MESH,
+        ).wait_recv()
+
+    @pl.when((half == 0) | (group == 0))
+    def _():
+        prev[0] = jnp.zeros((EDGE, LANES), F32)
+
+    def whole_states(side):
+        states = []
+        for o in range(MEMBERS):
+            own = got1[side, o, poles : poles + EDGE, :]
+            ahead = got1[side, o - 1, poles : poles + EDGE, :] if o else prev[side]
+            firsts, seconds = [], []
+            for i in range(2):
+                one = taps_ref[member, 2 * i : 2 * i + 1, :]
+                two = taps_ref[member, 2 * i + 1 : 2 * i + 2, :]
+                older, newer = ahead[4 + 2 * i : 5 + 2 * i, :], ahead[5 + 2 * i : 6 + 2 * i, :]
+                firsts.append(own[2 * i : 2 * i + 1, :] + one * newer + two * older)
+                seconds.append(own[2 * i + 1 : 2 * i + 2, :] + two * newer)
+            first = (firsts[0] * firsts[1]).astype(BF16).astype(F32)
+            second = (seconds[0] * seconds[1]).astype(BF16).astype(F32)
+            states.append(
+                got1[side, o, 0:poles, :] + apow[0, member] * first
+                + apow[3 + groups, member] * second
+            )
+        return states
+
+    def total(states):
         return (
-            got1[side, 3] + apow[0, member] * got1[side, 2]
-            + apow[1, member] * got1[side, 1] + apow[2, member] * got1[side, 0]
-        )
-
-    first_total = total(0)
-    own_total = total(1)
+            states[3] + apow[0, member] * states[2]
+            + apow[1, member] * states[1] + apow[2, member] * states[0]
+        )
+
+    first_total = total(whole_states(0))
+    own_states = whole_states(1)
+    own_total = total(own_states)
     gbuf[0] = own_total + apow[2 + groups, member] * first_total
     gbuf[1] = first_total
 
@@ -203,6 +297,19 @@
         copy.start()
         copies2.append(copy)
 
+    halo_copy.wait()
+    for i in range(3):
+        padded[i, PAD - 2 : PAD, :] = jnp.where(ctx > 0, halo[2 * i : 2 * i + 2, :], 0.0)
+    products(0, SUB)
+    inner_states([0])
+    for b in range(subs):
+        qs[b * SUB : (b + 1) * SUB, :] = short(2, 0, b * SUB, (b + 1) * SUB)
+    for l in range(quarters):
+        state = jnp.zeros((poles, LANES), F32)
+        for b in range(subs):
+            grown = prefix[b, l]
+            prefix[b, l] = state
+            state = state * dec_ref[l] + grown
     for l in range(quarters):
         lanes = slice(l * LANES, (l + 1) * LANES)
         sums = [jnp.zeros((SUB, LANES), F32) for _ in range(subs)]
@@ -218,11 +325,13 @@
         for b in range(subs):
             ylocal[b * SUB : (b + 1) * SUB, lanes] = sums[b]
 
-    inside = got1[1, 0]
+    inside = own_states[0]
     inner = [jnp.zeros((poles, LANES), F32), inside]
     for o in range(1, MEMBERS - 1):
-        inside = inside * apow[0, member] + got1[1, o]
+        inside = inside * apow[0, member] + own_states[o]
         inner.append(inside)
+    for o in range(1, MEMBERS):
+        cbuf[o] = inner[o]
     carry = apow[2 + groups - 1, member] * gbuf[1]
     for o in sorted(range(1, groups), key=lambda o: min(o, groups - o)):
         pltpu.make_async_remote_copy(
@@ -232,7 +341,7 @@
         carry = carry + (got2[o] if o == 1 else apow[2 + o - 1, member] * got2[o])
     cbuf[0] = carry
     for o in range(1, MEMBERS):
-        cbuf[o] = apow[o - 1, member] * carry + inner[o]
+        cbuf[o] = apow[o - 1, member] * carry + cbuf[o]
     got3[member] = cbuf[member]
     for o in range(1, MEMBERS):
         to = (member + o) % MEMBERS
@@ -249,7 +358,7 @@
 
     for l in range(quarters):
         lanes = slice(l * LANES, (l + 1) * LANES)
-        decay = jnp.exp(-rate_ref[:, lanes] * float(SUB))
+        decay = dec_ref[l]
         state = got3[l]
         for b in range(subs):
             carried[b, l] = state
@@ -266,6 +375,11 @@
 
     for copy in copies1 + copies2:
         copy.wait_send()
+    for due, copy in edge_sends:
+
+        @pl.when(due)
+        def _():
+            copy.wait_send()
 
     @pl.when(half == 0)
     def _():
@@ -294,6 +408,7 @@
     subs = tokens // SUB
     vmem = pltpu.VMEM
     state = (poles, LANES)
+    message = (poles + EDGE, LANES)
     dma = pltpu.SemaphoreType.DMA
     whole = pl.BlockSpec(memory_space=pltpu.VMEM)
     outside = pl.BlockSpec(memory_space=pltpu.HBM)
@@ -319,15 +434,19 @@
             vmem((tokens, width), F32),
             vmem((subs, quarters) + state, F32),
             vmem((subs, quarters) + state, F32),
-            vmem((3 + groups, quarters) + state, F32),
+            vmem((4 + groups, quarters) + state, F32),
+            vmem((quarters, 8, LANES), F32),
             vmem((quarters,) + state, F32),
-            vmem((2, MEMBERS) + state, F32),
+            vmem((quarters,) + message, F32),
+            vmem((2, MEMBERS) + message, F32),
+            vmem((2, EDGE, LANES), F32),
             vmem((2,) + state, F32),
             vmem((groups,) + state, F32),
             vmem((MEMBERS,) + state, F32),
             vmem((quarters,) + state, F32),
             dma((7,)), pltpu.SemaphoreType.REGULAR, dma, dma,
             dma((MEMBERS,)), dma((MEMBERS,)), dma((MEMBERS,)), dma((MEMBERS,)),
+            dma((MEMBERS,)), dma, dma((MEMBERS,)), dma,
             dma((groups,)), dma((groups,)), dma((MEMBERS,)), dma((MEMBERS,)),
         ],
         compiler_params=pltpu.CompilerParams(

time: 49.6 us -> 47.4 us (0.956)
  Pallas kernels: 47.9 us -> 45.6 us
    pallas_call x1, Pallas kernels: 47.9 us -> 45.6 us  [per_device(): pl.pallas_call(functools.partial(kernel, z_len, groups), out_shape=jax.Sh...]
where the time goes in v3:
time: 47.4 us; the launch traced here: 47.2 us
  Pallas kernels  45.6 us (96%)
  local copies, waits for them, and re-layouts  1.57 us (3%)
    pallas_call x1, Pallas kernels, per_device(): pl.pallas_call(functools.partial(kernel, z_len, groups), out_shape=jax.Sh...  45.6 us
    unnamed x1, local copies, waits for them, and re-layouts  1.57 us

profile of v3, /device:TPU:6, one launch (start us, length us, event | category | flops | bytes accessed | tf_op | source)
XLA Modules:
  0.0 47.2 jit_solution(4278157307757541458)
XLA Ops:
  0.0 45.6 %modal_scan.1 = bf16[128,512]{1,0:T(8,128)(2,1)} custom-call(bf16[128,512]{1,0:T(8,128)(2,1)} %q_hbm.1, bf16[128,512]{1,0:T(8,128)(2,1)} %k_hbm.1, bf16[128,512]{1,0:T(8,128)(2,1)} %v_hbm.1, f32[3,3,512]{2,1,0:T(4,128)} %cw_hbm.1, f32[16,512]{1,0:T(8,128)} %rate_hbm.1, f32[16,512]{1,0:T(8,128)} %res_hbm.1, f32[1,512]{1,0:T(1,128)} %bitcast.1), custom_call_target="tpu_custom_call" | custom-call | tf_op jit(solution)/shard_map/modal_scan/pallas_call | solution.py:415
  45.6 1.6 %copy.9 = bf16[128,512]{1,0:T(8,128)(2,1)} copy(bf16[128,512]{1,0:T(8,128)(2,1)} %modal_scan.1) | data formatting | bytes 262144

commit v4 on v3

--- a/solution.py
+++ b/solution.py
@@ -450,11 +450,14 @@
             dma((groups,)), dma((groups,)), dma((MEMBERS,)), dma((MEMBERS,)),
         ],
         compiler_params=pltpu.CompilerParams(
-            collective_id=0, has_side_effects=True, vmem_limit_bytes=67_043_328
+            collective_id=0, has_side_effects=True, vmem_limit_bytes=40 * 1024 * 1024
         ),
         name="modal_scan",
-    )(query_stream, key_stream, value_stream, conv_weight, decay_rates, residues,
-      skip_gain.reshape(1, width))
+    )(*[
+        pltpu.with_memory_space_constraint(operand, pltpu.HBM)
+        for operand in (query_stream, key_stream, value_stream, conv_weight, decay_rates,
+                        residues, skip_gain.reshape(1, width))
+    ])
 
 
 def solution(mesh):

time: 47.4 us -> 45.8 us (0.966)
  local copies, waits for them, and re-layouts: 1.57 us -> 0.66 us
  Pallas kernels: 45.6 us -> 45 us
    unnamed x1, local copies, waits for them, and re-layouts: 1.57 us -> 0.66 us
    pallas_call x1, Pallas kernels: 45.6 us -> 45 us  [per_device(): pl.pallas_call(functools.partial(kernel, z_len, groups), out_shape=jax.Sh...]
where the time goes in v4:
time: 45.8 us; the launch traced here: 45.6 us
  Pallas kernels  45 us (98%)
  local copies, waits for them, and re-layouts  0.66 us (1%)
    pallas_call x1, Pallas kernels, per_device(): pl.pallas_call(functools.partial(kernel, z_len, groups), out_shape=jax.Sh...  45 us

profile of v4, /device:TPU:6, one launch (start us, length us, event | category | flops | bytes accessed | tf_op | source)
XLA Modules:
  0.0 45.6 jit_solution(14427607361082039885)
XLA Ops:
  0.0 45.0 %modal_scan.1 = bf16[128,512]{1,0:T(8,128)(2,1)S(1)} custom-call(bf16[128,512]{1,0:T(8,128)(2,1)} %q_hbm.1, bf16[128,512]{1,0:T(8,128)(2,1)} %k_hbm.1, bf16[128,512]{1,0:T(8,128)(2,1)} %v_hbm.1, f32[3,3,512]{2,1,0:T(4,128)} %cw_hbm.1, f32[16,512]{1,0:T(8,128)} %rate_hbm.1, f32[16,512]{1,0:T(8,128)} %res_hbm.1, f32[1,512]{1,0:T(1,128)} %bitcast.1), custom_call_target="tpu_custom_call" | custom-call | tf_op jit(solution)/shard_map/modal_scan/pallas_call | solution.py:415
  45.0 0.7 %copy.9 = bf16[128,512]{1,0:T(8,128)(2,1)} copy(bf16[128,512]{1,0:T(8,128)(2,1)S(1)} %modal_scan.1) | data formatting | bytes 262144

commit v5 on v4

--- a/solution.py
+++ b/solution.py
@@ -189,14 +189,6 @@
     )
     halo_copy.start()
 
-    steps = lax.broadcasted_iota(jnp.int32, (SUB, width), 0).astype(F32)
-    taps = jnp.zeros((SUB, width), F32)
-    for n in range(poles):
-        row = res_ref[n : n + 1, :] * jnp.exp(-rate_ref[n : n + 1, :] * steps)
-        etab[n] = row
-        taps = taps + row
-    hpad[0:SUB, :] = jnp.zeros((SUB, width), F32)
-    hpad[SUB:, :] = taps
     for l in range(quarters):
         rates = rate_ref[:, l * LANES : (l + 1) * LANES]
         for i, power in enumerate((1, 2, 3) + tuple(range(4, 4 * groups + 1, 4))):
@@ -208,8 +200,6 @@
         apow[3 + groups, l] = jnp.exp(-rates * float(tokens - 1))
         for i in range(2):
             taps_ref[l, 2 * i : 2 * i + 2, :] = cw_ref[i + 1, 1:3, lanes]
-    for s in range(SUB):
-        htab[s] = hpad[SUB - s : 2 * SUB - s, :]
 
     got1[1, member] = tbuf[member]
     for o in range(1, MEMBERS):
@@ -296,6 +286,17 @@
         )
         copy.start()
         copies2.append(copy)
+
+    steps = lax.broadcasted_iota(jnp.int32, (SUB, width), 0).astype(F32)
+    taps = jnp.zeros((SUB, width), F32)
+    for n in range(poles):
+        row = res_ref[n : n + 1, :] * jnp.exp(-rate_ref[n : n + 1, :] * steps)
+        etab[n] = row
+        taps = taps + row
+    hpad[0:SUB, :] = jnp.zeros((SUB, width), F32)
+    hpad[SUB:, :] = taps
+    for s in range(SUB):
+        htab[s] = hpad[SUB - s : 2 * SUB - s, :]
 
     halo_copy.wait()
     for i in range(3):

time: 45.8 us -> 45.8 us (level)
  no operation moved by 1% of the time
where the time goes in v5:
time: 45.8 us; the launch traced here: 45.6 us
  Pallas kernels  45 us (98%)
  local copies, waits for them, and re-layouts  0.66 us (1%)
    pallas_call x1, Pallas kernels, per_device(): pl.pallas_call(functools.partial(kernel, z_len, groups), out_shape=jax.Sh...  45 us

profile of v5, /device:TPU:6, one launch (start us, length us, event | category | flops | bytes accessed | tf_op | source)
XLA Modules:
  0.0 45.6 jit_solution(17639992682357283840)
XLA Ops:
  0.0 45.0 %modal_scan.1 = bf16[128,512]{1,0:T(8,128)(2,1)S(1)} custom-call(bf16[128,512]{1,0:T(8,128)(2,1)} %q_hbm.1, bf16[128,512]{1,0:T(8,128)(2,1)} %k_hbm.1, bf16[128,512]{1,0:T(8,128)(2,1)} %v_hbm.1, f32[3,3,512]{2,1,0:T(4,128)} %cw_hbm.1, f32[16,512]{1,0:T(8,128)} %rate_hbm.1, f32[16,512]{1,0:T(8,128)} %res_hbm.1, f32[1,512]{1,0:T(1,128)} %bitcast.1), custom_call_target="tpu_custom_call" | custom-call | tf_op jit(solution)/shard_map/modal_scan/pallas_call | solution.py:416
  45.0 0.7 %copy.9 = bf16[128,512]{1,0:T(8,128)(2,1)} copy(bf16[128,512]{1,0:T(8,128)(2,1)S(1)} %modal_scan.1) | data formatting | bytes 262144
